TPU v7x, 32 devices: a whole 2x2x4 slice. The times are simulated.
32 devices in a mesh: term: 8 (over z, core), doc: 4 (over y, x).
Axes of the slice: x: 2, y: 2, z: 4, core: 2. Of those that a mesh axis runs over, the one named last changes fastest.
Arguments:
- tile_values: bfloat16 [384, 512, 128], P('term', 'doc'), may hold values from 0.001 to 1, as said below
- tile_rows: int32 [8, 192], P('term', 'doc'), may hold values from 0 to 15, as said below
- tile_cols: int32 [8, 192], P('term', 'doc'), may hold values from 0 to 15, as said below
- tile_count: int32 [8, 4], P('term', 'doc'), may hold values from 16 to 48, as said below
- start_block: bfloat16 [8192, 256], P('doc'), may hold values from -6 to 6
Outputs:
- row_scale: float32 [16384], P('term')
- col_scale: float32 [8192], P('doc')
- left_basis: bfloat16 [16384, 256], P('term')
- right_basis: bfloat16 [8192, 256], P('doc')
Inputs may be any that keep to these rules, and one draw needn't show every extreme that they name: `tile_values`: entries are positive. `tile_rows`: within one block pair the occupied (row, column) pairs are distinct, and every tile row and tile column of every block pair holds an occupied tile. `tile_cols`: paired with tile_rows slot by slot. `tile_count`: some block pair has all 48 slots occupied.
All inputs are finite; a program needn't handle non-finite values.
Results may differ from a plain program's by a relative error of at most 0.006.
The roundings to bfloat16 on the way count: a program that leaves them out, or rounds other values in their place, can miss the bound.
Values may be sent and summed in bfloat16 or wider, within the bound.
A program may use at most 64 MiB of HBM per device.

v0:
```python
import math
import jax
import jax.numpy as jnp
from jax import lax
from jax.sharding import PartitionSpec as P

TILE = 128
K = 256
PASSES = 2
RB = 16
CB = 16
PRECISE = lax.Precision.HIGHEST


def factor_inverse(gram):
    lower = jnp.linalg.cholesky(gram)
    identity = jnp.eye(gram.shape[0], dtype=gram.dtype)
    return jax.scipy.linalg.solve_triangular(lower, identity, lower=True).T


def over_tiles(tile_values, row_ids, col_ids, occupied, advance, initial):
    slot_total = tile_values.shape[0]
    group_size = math.gcd(slot_total, 32)

    def visit(turn_index, running):
        offset = turn_index * group_size
        tile_block = lax.dynamic_slice_in_dim(tile_values, offset, group_size, 0)
        row_block = lax.dynamic_slice_in_dim(row_ids, offset, group_size, 0)
        col_block = lax.dynamic_slice_in_dim(col_ids, offset, group_size, 0)
        live_mask = (offset + jnp.arange(group_size, dtype=jnp.int32) < occupied).astype(
            jnp.float32
        )
        return advance(running, tile_block, row_block, col_block, live_mask)

    turn_total = slot_total // group_size
    return lax.fori_loop(0, turn_total, visit, initial)


def row_vector(source):

    def advance(running, tile_block, row_block, col_block, live_mask):
        picked = jnp.take(source, col_block, axis=0)
        product = jnp.einsum(
            "gab,gb->ga", tile_block.astype(jnp.float32), picked, precision=PRECISE
        )
        return running.at[row_block].add(product * live_mask[:, None])

    return advance


def col_vector(source):

    def advance(running, tile_block, row_block, col_block, live_mask):
        picked = jnp.take(source, row_block, axis=0)
        product = jnp.einsum(
            "gab,ga->gb", tile_block.astype(jnp.float32), picked, precision=PRECISE
        )
        return running.at[col_block].add(product * live_mask[:, None])

    return advance


def row_matrix(source):

    def advance(running, tile_block, row_block, col_block, live_mask):
        picked = jnp.take(source, col_block, axis=0)
        product = jnp.einsum("gab,gbk->gak", tile_block, picked, preferred_element_type=jnp.float32)
        return running.at[row_block].add(product * live_mask[:, None, None])

    return advance


def col_matrix(source):

    def advance(running, tile_block, row_block, col_block, live_mask):
        picked = jnp.take(source, row_block, axis=0)
        product = jnp.einsum("gab,gak->gbk", tile_block, picked, preferred_element_type=jnp.float32)
        return running.at[col_block].add(product * live_mask[:, None, None])

    return advance


def per_device(tile_values, tile_rows, tile_cols, tile_count, start_block):
    row_list = tile_rows[0]
    col_list = tile_cols[0]
    occupied = tile_count[0, 0]
    terms_total = RB * TILE * lax.axis_size("term")
    docs_total = CB * TILE * lax.axis_size("doc")

    def tile_pass(advance, initial):
        return over_tiles(tile_values, row_list, col_list, occupied, advance, initial)

    col_scale = jnp.ones((CB, TILE), jnp.float32)
    row_scale = jnp.ones((RB, TILE), jnp.float32)
    mean_part = jnp.sum(start_block.astype(jnp.float32), axis=0)
    start_mean = mean_part
    for sweep_index in range(PASSES):
        row_part = tile_pass(row_vector(col_scale), jnp.zeros((RB, TILE), jnp.float32))
        if sweep_index == 0:
            row_total, start_mean = lax.psum((row_part, mean_part), "doc")
        else:
            row_total = lax.psum(row_part, "doc")
        row_scale = 1.0 / row_total
        col_part = tile_pass(col_vector(row_scale), jnp.zeros((CB, TILE), jnp.float32))
        col_scale = 1.0 / lax.psum(col_part, "term")
    weight_part = tile_pass(row_vector(col_scale), jnp.zeros((RB, TILE), jnp.float32)).reshape(-1)
    row_flat = row_scale.reshape(-1)
    col_flat = col_scale.reshape(-1)
    scaled_start = (col_flat[:, None] * start_block.astype(jnp.float32)).astype(jnp.bfloat16)
    left_part = tile_pass(
        row_matrix(scaled_start.reshape(CB, TILE, K)), jnp.zeros((RB, TILE, K), jnp.float32)
    )
    left_part = left_part.reshape(RB * TILE, K)
    left_share = RB * TILE // lax.axis_size("doc")
    left_offset = lax.axis_index("doc") * left_share
    left_raw, weight_sum = (
        lax.psum_scatter(left_part, "doc", scatter_dimension=0, tiled=True),
        lax.psum_scatter(weight_part, "doc", scatter_dimension=0, tiled=True),
    )
    row_rows = lax.dynamic_slice_in_dim(row_flat, left_offset, left_share)
    row_weight = row_rows * weight_sum
    left_block = (
        row_rows[:, None] * left_raw - row_weight[:, None] * start_mean[None, :] / docs_total
    )
    gram_part = jnp.dot(left_block.T, left_block, precision=PRECISE) / terms_total
    left_gram = lax.psum(gram_part, ("term", "doc"))
    left_inverse = factor_inverse(left_gram)
    share_float = jnp.dot(left_block, left_inverse, precision=PRECISE)
    lean = lax.psum(jnp.dot(row_weight, share_float, precision=PRECISE), ("term", "doc"))
    left_basis = lax.all_gather(share_float.astype(jnp.bfloat16), "doc", axis=0, tiled=True)
    scaled_left = (row_flat[:, None] * left_basis.astype(jnp.float32)).astype(jnp.bfloat16)
    right_part = tile_pass(
        col_matrix(scaled_left.reshape(RB, TILE, K)), jnp.zeros((CB, TILE, K), jnp.float32)
    )
    right_part = right_part.reshape(CB * TILE, K)
    right_share = CB * TILE // lax.axis_size("term")
    right_offset = lax.axis_index("term") * right_share
    right_raw = lax.psum_scatter(right_part, "term", scatter_dimension=0, tiled=True)
    col_rows = lax.dynamic_slice_in_dim(col_flat, right_offset, right_share)
    right_block = col_rows[:, None] * right_raw - lean[None, :] / docs_total
    right_gram = lax.psum(
        jnp.dot(right_block.T, right_block, precision=PRECISE) / docs_total, ("term", "doc")
    )
    right_inverse = factor_inverse(right_gram)
    right_piece = jnp.dot(right_block, right_inverse, precision=PRECISE).astype(jnp.bfloat16)
    right_basis = lax.all_gather(right_piece, "term", axis=0, tiled=True)
    return (row_flat, col_flat, left_basis, right_basis)


def solution(mesh):
    placed = (
        P("term", "doc", None),
        P("term", "doc"),
        P("term", "doc"),
        P("term", "doc"),
        P("doc", None),
    )
    return jax.shard_map(
        per_device,
        mesh=mesh,
        in_specs=placed,
        out_specs=(P("term"), P("doc"), P("term", None), P("doc", None)),
        check_vma=False,
    )
```

profile of v0, /device:TPU:0, one launch (start us, length us, event | category | flops | bytes accessed | tf_op | source)
XLA Modules:
  0.0 707.7 jit_solution(8879846840978925961)
XLA Ops:
  7.2 16.4 %while.95 = (s32[]{:T(128)}, f32[16,128]{1,0:T(8,128)S(1)}, s32[48]{0:T(128)}, bf16[48,128,128]{2,1,0:T(8,128)(2,1)}, s32[48]{0:T(128)}, /*index=5*/s32[]{:T(128...) while((s32[]{:T(128)}, f32[16,128]{1,0:T(8,128)S(1)}, s32[48]{0:T(128)}, ...), condition=%wide.region_2.4_spmd, body=%wide.region_0.3_spmd.sunk | while | flops 3153094 | bytes 603283 | solution.py:36
  10.0 1.9 fusion.133
  15.5 1.9 fusion.133
  20.9 1.9 fusion.133
  23.6 11.5 %psum.56 = f32[16,128]{1,0:T(8,128)S(1)} all-reduce(f32[16,128]{1,0:T(8,128)S(1)} %get-tuple-element.861), channel_id=1, replica_groups=mesh['term'=8,'doc'=4] {'doc'}, use_global_device_ids=true, to_apply=%region_3.0 | all-reduce | flops 2048 | bytes 16384 | tf_op jit(solution)/shard_map/psum | solution.py:100
  35.2 15.1 %while.96 = (s32[]{:T(128)}, f32[16,128]{1,0:T(8,128)S(1)}, s32[48]{0:T(128)}, bf16[48,128,128]{2,1,0:T(8,128)(2,1)}, s32[48]{0:T(128)}, /*index=5*/f32[16,128]{...) while((s32[]{:T(128)}, f32[16,128]{1,0:T(8,128)S(1)}, s32[48]{0:T(128)}, ...), condition=%wide.region_6.8_spmd, body=%wide.region_4.0_spmd.sunk | while | flops 3153094 | bytes 595087 | solution.py:36
  38.0 1.6 fusion.137
  43.0 1.6 fusion.137
  48.1 1.6 fusion.137
  50.3 15.0 %psum.57 = f32[16,128]{1,0:T(8,128)S(1)} all-reduce(f32[16,128]{1,0:T(8,128)S(1)} %get-tuple-element.862), channel_id=1, replica_groups=mesh['term'=8,'doc'=4] {'term'}, use_global_device_ids=true, to_apply=%region_7.9 | all-reduce | flops 2048 | bytes 16384 | tf_op jit(solution)/shard_map/psum | solution.py:105
  65.4 16.4 %while.97 = (s32[]{:T(128)}, f32[16,128]{1,0:T(8,128)S(1)}, s32[48]{0:T(128)}, bf16[48,128,128]{2,1,0:T(8,128)(2,1)}, s32[48]{0:T(128)}, /*index=5*/f32[16,128]{...) while((s32[]{:T(128)}, f32[16,128]{1,0:T(8,128)S(1)}, s32[48]{0:T(128)}, ...), condition=%wide.region_10.12_spmd, body=%wide.region_8.11_spmd.sunk | while | flops 3153094 | bytes 595087 | solution.py:36
  68.3 1.9 fusion.141
  73.7 1.9 fusion.141
  79.2 1.9 fusion.141
  81.9 8.2 %psum.58 = f32[16,128]{1,0:T(8,128)S(1)} all-reduce(f32[16,128]{1,0:T(8,128)S(1)} %get-tuple-element.863), channel_id=1, replica_groups=mesh['term'=8,'doc'=4] {'doc'}, use_global_device_ids=true, to_apply=%region_11.13 | all-reduce | flops 2048 | bytes 16384 | tf_op jit(solution)/shard_map/psum | solution.py:102
  90.1 15.1 %while.98 = (s32[]{:T(128)}, f32[16,128]{1,0:T(8,128)S(1)}, s32[48]{0:T(128)}, bf16[48,128,128]{2,1,0:T(8,128)(2,1)}, s32[48]{0:T(128)}, /*index=5*/f32[16,128]{...) while((s32[]{:T(128)}, f32[16,128]{1,0:T(8,128)S(1)}, s32[48]{0:T(128)}, ...), condition=%wide.region_14.16_spmd, body=%wide.region_12.15_spmd.sunk | while | flops 3153094 | bytes 595087 | solution.py:36
  92.9 1.6 fusion.145
  97.9 1.6 fusion.145
  103.0 1.6 fusion.145
  105.2 13.9 %psum.59 = f32[16,128]{1,0:T(8,128)S(1)} all-reduce(f32[16,128]{1,0:T(8,128)S(1)} %get-tuple-element.864), channel_id=1, replica_groups=mesh['term'=8,'doc'=4] {'term'}, use_global_device_ids=true, to_apply=%region_15.17 | all-reduce | flops 2048 | bytes 16384 | tf_op jit(solution)/shard_map/psum | solution.py:105
  120.7 1.6 broadcast.307.clone
  122.3 29.0 %while.99 = (s32[]{:T(128)}, f32[16,128,256]{2,1,0:T(8,128)}, s32[48]{0:T(128)S(1)}, bf16[48,128,128]{2,1,0:T(8,128)(2,1)S(1)}, s32[48]{0:T(128)S(1)}, /*index=5...) while((s32[]{:T(128)}, f32[16,128,256]{2,1,0:T(8,128)}, ...), condition=%wide.region_18.0_spmd, body=%wide.region_16.20_spmd.sunk | while | flops 135791808 | bytes 12064447 | solution.py:36
  123.1 1.8 gather_fusion.4
  125.0 1.8 convolution_multiply_fusion.6
  126.8 5.4 scatter_fusion
  133.0 1.8 gather_fusion.4
  134.8 1.8 convolution_multiply_fusion.6
  136.6 5.2 scatter_fusion
  142.6 1.8 gather_fusion.4
  144.5 1.8 convolution_multiply_fusion.6
  146.3 5.0 scatter_fusion
  153.1 9.3 %while.100 = (s32[]{:T(128)}, f32[16,128]{1,0:T(8,128)S(1)}, s32[48]{0:T(128)S(1)}, bf16[48,128,128]{2,1,0:T(8,128)(2,1)S(1)}, s32[48]{0:T(128)S(1)}, /*index=5*...) while((s32[]{:T(128)}, f32[16,128]{1,0:T(8,128)S(1)}, ...), condition=%wide.region_22.25_spmd, body=%wide.region_20.24_spmd.sunk | while | flops 3153094 | bytes 595087 | solution.py:36
  162.5 9.6 %all-reduce.2 = (f32[256]{0:T(256)S(1)}, f32[2048]{0:T(1024)S(1)}) all-reduce(f32[256]{0:T(256)S(1)} %get-tuple-element.1039, f32[2048]{0:T(1024)S(1)} %bitcast.155), channel_id=1, replica_groups=mesh['term'=8,'doc'=4] {'doc'}, use_global_device_ids=true, to_apply=%region_25.28 | all-reduce | flops 2304 | bytes 18432 | tf_op jit(solution)/shard_map/psum | solution.py:100
  172.1 12.6 %reduce-scatter.3.cloned.1.call-done = f32[512,256]{1,0:T(8,128)} async-done(((f32[2048,256]{1,0:T(8,128)}), f32[512,256]{1,0:T(8,128)}) %reduce-scatter.3.cloned.1.call-update) | async-done | bytes 524304 | tf_op jit(solution)/shard_map/reduce_scatter | solution.py:117
  184.8 3.2 convolution_multiply_fusion.3
  188.6 128.9 %all-reduce.6.cloned.1.call-done = f32[256,256]{0,1:T(8,128)} async-done(((f32[256,256]{0,1:T(8,128)}), f32[256,256]{0,1:T(8,128)}) %all-reduce.6.cloned.1.call-update) | async-done | bytes 262160 | tf_op jit(solution)/shard_map/psum | solution.py:126
  319.6 11.7 %cholesky.130 = f32[128,128]{1,0:T(8,128)S(1)} custom-call(f32[128,128]{1,0:T(8,128)S(1)} %cholesky.194), custom_call_target="Cholesky" | custom-call | tf_op jit(solution)/shard_map/jit(cholesky)/cholesky | solution.py:16
  331.4 9.8 %custom-call.13 = f32[1,128,128]{1,2,0:T(8,128)S(1)} custom-call(f32[1,128,128]{2,1,0:T(8,128)S(1)} %get-tuple-element.1048), custom_call_target="InvertDiagBlocksLowerTriangular" | custom-call | tf_op jit(solution)/shard_map/jit(cholesky)/cholesky | solution.py:16
  341.7 11.7 %cholesky.147 = f32[128,128]{1,0:T(8,128)S(1)} custom-call(f32[128,128]{1,0:T(8,128)S(1)} %convolution_subtract_fusion.3), custom_call_target="Cholesky" | custom-call | tf_op jit(solution)/shard_map/jit(cholesky)/cholesky | solution.py:16
  355.6 4.3 while.102
  359.9 19.7 %custom-call.14 = f32[2,128,128]{1,2,0:T(8,128)S(1)} custom-call(f32[2,128,128]{2,1,0:T(8,128)S(1)} %get-tuple-element.882), custom_call_target="InvertDiagBlocksLowerTriangular" | custom-call | tf_op jit(solution)/shard_map/jit(_solve_triangular)/triangular_solve | solution.py:18
  380.5 2.4 fusion.87
  383.0 25.7 %all-gather.3.cloned.1.call-done = bf16[2048,256]{1,0:T(8,128)(2,1)} async-done(((bf16[512,256]{1,0:T(8,128)(2,1)}), bf16[2048,256]{1,0:T(8,128)(2,1)}) %all-gather.3.cloned.1.call-update) | async-done | bytes 1048592 | tf_op jit(solution)/shard_map/all_gather | solution.py:130
  408.6 2.5 multiply_convert_fusion
  411.2 1.6 broadcast.307
  412.7 29.1 %while.101 = (s32[]{:T(128)}, f32[16,128,256]{2,1,0:T(8,128)}, s32[48]{0:T(128)S(1)}, bf16[48,128,128]{2,1,0:T(8,128)(2,1)S(1)}, s32[48]{0:T(128)S(1)}, /*index=...) while((s32[]{:T(128)}, f32[16,128,256]{2,1,0:T(8,128)}, ...), condition=%wide.region_33.38_spmd, body=%wide.region_31.37_spmd.sunk | while | flops 135791808 | bytes 12064447 | solution.py:36
  413.5 1.8 gather_fusion.6
  415.4 1.8 convolution_multiply_fusion.7
  417.2 5.4 scatter_fusion.1
  423.4 1.8 gather_fusion.6
  425.3 1.8 convolution_multiply_fusion.7
  427.1 5.1 scatter_fusion.1
  433.0 1.8 gather_fusion.6
  434.8 1.8 convolution_multiply_fusion.7
  436.6 5.2 scatter_fusion.1
  442.3 40.0 %psum.62 = f32[256]{0:T(256)S(1)} all-reduce(f32[256]{0:T(256)S(1)} %bitcast.157), channel_id=1, replica_groups=mesh['term'=8,'doc'=4] {'term','doc'}, use_global_device_ids=true, to_apply=%region_35.40 | all-reduce | flops 256 | bytes 2048 | tf_op jit(solution)/shard_map/psum | solution.py:129
  482.3 2.4 convolution_multiply_fusion.2
  485.0 127.2 %all-reduce.8.cloned.1.call-done = f32[256,256]{0,1:T(8,128)} async-done(((f32[256,256]{0,1:T(8,128)}), f32[256,256]{0,1:T(8,128)}) %all-reduce.8.cloned.1.call-update) | async-done | bytes 262160 | tf_op jit(solution)/shard_map/psum | solution.py:141
  614.4 11.7 %cholesky.164 = f32[128,128]{1,0:T(8,128)S(1)} custom-call(f32[128,128]{1,0:T(8,128)S(1)} %cholesky.197), custom_call_target="Cholesky" | custom-call | tf_op jit(solution)/shard_map/jit(cholesky)/cholesky | solution.py:16
  626.8 9.8 %custom-call.15 = f32[1,128,128]{1,2,0:T(8,128)S(1)} custom-call(f32[1,128,128]{2,1,0:T(8,128)S(1)} %get-tuple-element.1044), custom_call_target="InvertDiagBlocksLowerTriangular" | custom-call | tf_op jit(solution)/shard_map/jit(cholesky)/cholesky | solution.py:16
  637.1 11.7 %cholesky.181 = f32[128,128]{1,0:T(8,128)S(1)} custom-call(f32[128,128]{1,0:T(8,128)S(1)} %convolution_subtract_fusion.2), custom_call_target="Cholesky" | custom-call | tf_op jit(solution)/shard_map/jit(cholesky)/cholesky | solution.py:16
  650.7 4.1 while.103
  654.8 19.7 %custom-call.16 = f32[2,128,128]{1,2,0:T(8,128)S(1)} custom-call(f32[2,128,128]{2,1,0:T(8,128)S(1)} %get-tuple-element.883), custom_call_target="InvertDiagBlocksLowerTriangular" | custom-call | tf_op jit(solution)/shard_map/jit(_solve_triangular)/triangular_solve | solution.py:18
  676.5 21.4 %all-gather.5.cloned.1.call-done = bf16[2048,256]{1,0:T(8,128)(2,1)} async-done(((bf16[256,256]{1,0:T(8,128)(2,1)}), bf16[2048,256]{1,0:T(8,128)(2,1)}) %all-gather.5.cloned.1.call-update) | async-done | bytes 1048592 | tf_op jit(solution)/shard_map/all_gather | solution.py:146
  (209 shorter events, 80.7 us)
Async XLA Ops:
  7.2 177.6 %reduce-scatter.3.cloned.1.call-start = ((), (), s32[]{:S(2)}) async-start(), calls=%async_computation.2 | async-start | bytes 2621440 | tf_op jit(solution)/shard_map/reduce_scatter | solution.py:117
  65.4 53.8 %copy-start.4 = (bf16[2048,256]{1,0:T(8,128)(2,1)S(1)}, bf16[2048,256]{1,0:T(8,128)(2,1)}, u32[]{:S(2)}) copy-start(bf16[2048,256]{1,0:T(8,128)(2,1)} %param.30) | copy-start | bytes 3145732
  90.1 318.6 %copy-start.7 = (f32[2048]{0:T(1024)}, f32[2048]{0:T(1024)S(1)}, u32[]{:S(2)}) copy-start(f32[2048]{0:T(1024)S(1)} %get-tuple-element.1721) | copy-start | bytes 24580
  119.2 322.8 %copy-start.8 = (f32[2048]{0:T(1024)}, f32[2048]{0:T(1024)S(1)}, u32[]{:S(2)}) copy-start(f32[2048]{0:T(1024)S(1)} %get-tuple-element.1722) | copy-start | bytes 24580
  119.2 3.1 copy-start
  119.2 3.1 copy-start.5
  119.2 3.1 copy-start.6
  151.3 0.7 copy-start.9
  151.3 166.2 %all-reduce.6.cloned.1.call-start = ((), (), s32[]{:S(2)}) async-start(), calls=%async_computation.3 | async-start | bytes 524288 | tf_op jit(solution)/shard_map/psum | solution.py:126
  188.0 220.6 %all-gather.3.cloned.1.call-start = ((), (), s32[]{:S(2)}) async-start(), calls=%async_computation.4 | async-start | bytes 1310720 | tf_op jit(solution)/shard_map/all_gather | solution.py:130
  382.9 99.4 %reduce-scatter.5.cloned.1.call-start = ((), (), s32[]{:S(2)}) async-start(), calls=%async_computation.5 | async-start | bytes 2359296 | tf_op jit(solution)/shard_map/reduce_scatter | solution.py:138
  441.9 170.4 %all-reduce.8.cloned.1.call-start = ((), (), s32[]{:S(2)}) async-start(), calls=%async_computation.6 | async-start | bytes 524288 | tf_op jit(solution)/shard_map/psum | solution.py:141
  484.8 213.2 %all-gather.5.cloned.1.call-start = ((), (), s32[]{:S(2)}) async-start(), calls=%async_computation.7 | async-start | bytes 1179648 | tf_op jit(solution)/shard_map/all_gather | solution.py:146
  614.3 61.1 %copy-start.3 = (f32[256,256]{1,0:T(8,128)S(1)}, f32[256,256]{1,0:T(8,128)}, u32[]{:S(2)}) copy-start(f32[256,256]{1,0:T(8,128)} %reduce-scatter.5.cloned.1.call-done) | copy-start | bytes 786436
  636.6 61.4 %copy-start.1 = (bf16[2048,256]{1,0:T(8,128)(2,1)S(1)}, bf16[2048,256]{1,0:T(8,128)(2,1)}, u32[]{:S(2)}) copy-start(bf16[2048,256]{1,0:T(8,128)(2,1)} %all-gather.3.cloned.1.call-done) | copy-start | bytes 3145732
  698.0 1.6 copy-start.2
Sparse Core Ops, SparseCore 0:
  151.4 33.2 reduce-scatter.2
  190.8 126.6 all-reduce.5
  383.0 25.5 all-gather.2
  442.0 36.4 reduce-scatter.4
  484.9 127.3 all-reduce.7
  676.6 21.2 all-gather.4
where the time goes:
time: 715 us; the launch traced here: 708 us
  waiting for transfers between devices  316 us (44%)
  other arithmetic  190 us (27%)
  blocking collectives  98.3 us (14%)
  matrix products  46.6 us (7%)
  local copies, waits for them, and re-layouts  36.6 us (5%)
  between operations  18 us (3%)
    psum x1, waiting for transfers between devices, per_device(): left_gram = lax.psum(gram_part, ('term', 'doc'))  129 us
    psum x1, waiting for transfers between devices, per_device(): lax.psum(jnp.dot(right_block.T, right_block, precision=PRECISE) / docs_to...  127 us
    another operation x13, other arithmetic, factor_inverse(): lower = jnp.linalg.cholesky(gram)  68.6 us
    psum x1, blocking collectives, per_device(): lax.psum(jnp.dot(row_weight, share_float, precision=PRECISE), ('term', 'd...  40 us
    another operation x5, other arithmetic, factor_inverse(): return jax.scipy.linalg.solve_triangular(lower, identity, lower=True).T  39.4 us
    psum x2, blocking collectives, per_device(): col_scale = 1.0 / lax.psum(col_part, 'term')  29 us
    all_gather x1, waiting for transfers between devices, per_device(): lax.all_gather(share_float.astype(jnp.bfloat16), 'doc', axis=0, tiled=True)  25.7 us
    all_gather x1, waiting for transfers between devices, per_device(): right_basis = lax.all_gather(right_piece, 'term', axis=0, tiled=True)  21.4 us
  transfers between devices with their start and end apart: 6, of which 5 were waited for; matrix products, arithmetic and copies ran while one was open for 1% of the time, Pallas kernels for 0%

commit v1 on v0

--- a/solution.py
+++ b/solution.py
@@ -138,8 +138,11 @@
     right_raw = lax.psum_scatter(right_part, "term", scatter_dimension=0, tiled=True)
     col_rows = lax.dynamic_slice_in_dim(col_flat, right_offset, right_share)
     right_block = col_rows[:, None] * right_raw - lean[None, :] / docs_total
-    right_gram = lax.psum(
-        jnp.dot(right_block.T, right_block, precision=PRECISE) / docs_total, ("term", "doc")
+    right_gram = jnp.sum(
+        lax.all_gather(
+            jnp.dot(right_block.T, right_block, precision=PRECISE) / docs_total, ("term", "doc")
+        ),
+        axis=0,
     )
     right_inverse = factor_inverse(right_gram)
     right_piece = jnp.dot(right_block, right_inverse, precision=PRECISE).astype(jnp.bfloat16)

time: 715 us -> 668 us (0.934)
  waiting for transfers between devices: 316 us -> 266 us
    psum x1 -> x0, waiting for transfers between devices: 127 us -> none  [per_device(): lax.psum(jnp.dot(right_block.T, right_block, precision=PRECISE) / docs_to...]
    all_gather x0 -> x1, waiting for transfers between devices: none -> 77.8 us  [per_device(): lax.all_gather(jnp.dot(right_block.T, right_block, precision=PRECISE) / d...]
  transfers between devices with their start and end apart: 6 -> 6, of which waited for: 5 -> 5; matrix products, arithmetic and copies ran while one was open for 1% -> 2% of each run, Pallas kernels for 0% -> 0%
where the time goes in v1:
time: 668 us; the launch traced here: 660 us
  waiting for transfers between devices  266 us (40%)
  other arithmetic  193 us (29%)
  blocking collectives  98.2 us (15%)
  matrix products  46.6 us (7%)
  local copies, waits for them, and re-layouts  36 us (5%)
  between operations  18.2 us (3%)
    psum x1, waiting for transfers between devices, per_device(): left_gram = lax.psum(gram_part, ('term', 'doc'))  129 us
    all_gather x1, waiting for transfers between devices, per_device(): lax.all_gather(jnp.dot(right_block.T, right_block, precision=PRECISE) / d...  77.8 us
    another operation x13, other arithmetic, factor_inverse(): lower = jnp.linalg.cholesky(gram)  68.7 us
    psum x1, blocking collectives, per_device(): lax.psum(jnp.dot(row_weight, share_float, precision=PRECISE), ('term', 'd...  40 us
    another operation x5, other arithmetic, factor_inverse(): return jax.scipy.linalg.solve_triangular(lower, identity, lower=True).T  39.4 us
    psum x2, blocking collectives, per_device(): col_scale = 1.0 / lax.psum(col_part, 'term')  29 us
    all_gather x1, waiting for transfers between devices, per_device(): lax.all_gather(share_float.astype(jnp.bfloat16), 'doc', axis=0, tiled=True)  25.6 us
    psum x2, blocking collectives, per_device(): row_total, start_mean = lax.psum((row_part, mean_part), 'doc')  21.1 us
  transfers between devices with their start and end apart: 6, of which 5 were waited for; matrix products, arithmetic and copies ran while one was open for 2% of the time, Pallas kernels for 0%

profile of v1, /device:TPU:0, one launch (start us, length us, event | category | flops | bytes accessed | tf_op | source)
XLA Modules:
  0.0 660.2 jit_solution(8236298438660941260)
XLA Ops:
  7.2 16.4 %while.95 = (s32[]{:T(128)}, f32[16,128]{1,0:T(8,128)S(1)}, s32[48]{0:T(128)}, bf16[48,128,128]{2,1,0:T(8,128)(2,1)}, s32[48]{0:T(128)}, /*index=5*/s32[]{:T(128...) while((s32[]{:T(128)}, f32[16,128]{1,0:T(8,128)S(1)}, s32[48]{0:T(128)}, ...), condition=%wide.region_2.4_spmd, body=%wide.region_0.3_spmd.sunk | while | flops 3153094 | bytes 603283 | solution.py:36
  9.3 1.9 fusion.133
  14.7 1.9 fusion.133
  20.2 1.9 fusion.133
  23.6 11.5 %psum.49 = f32[16,128]{1,0:T(8,128)S(1)} all-reduce(f32[16,128]{1,0:T(8,128)S(1)} %get-tuple-element.861), channel_id=1, replica_groups=mesh['term'=8,'doc'=4] {'doc'}, use_global_device_ids=true, to_apply=%region_3.0 | all-reduce | flops 2048 | bytes 16384 | tf_op jit(solution)/shard_map/psum | solution.py:100
  35.2 15.1 %while.96 = (s32[]{:T(128)}, f32[16,128]{1,0:T(8,128)S(1)}, s32[48]{0:T(128)}, bf16[48,128,128]{2,1,0:T(8,128)(2,1)}, s32[48]{0:T(128)}, /*index=5*/f32[16,128]{...) while((s32[]{:T(128)}, f32[16,128]{1,0:T(8,128)S(1)}, s32[48]{0:T(128)}, ...), condition=%wide.region_6.8_spmd, body=%wide.region_4.0_spmd.sunk | while | flops 3153094 | bytes 595087 | solution.py:36
  37.2 1.6 fusion.137
  42.3 1.6 fusion.137
  47.3 1.6 fusion.137
  50.3 15.0 %psum.50 = f32[16,128]{1,0:T(8,128)S(1)} all-reduce(f32[16,128]{1,0:T(8,128)S(1)} %get-tuple-element.862), channel_id=1, replica_groups=mesh['term'=8,'doc'=4] {'term'}, use_global_device_ids=true, to_apply=%region_7.9 | all-reduce | flops 2048 | bytes 16384 | tf_op jit(solution)/shard_map/psum | solution.py:105
  65.4 16.4 %while.97 = (s32[]{:T(128)}, f32[16,128]{1,0:T(8,128)S(1)}, s32[48]{0:T(128)}, bf16[48,128,128]{2,1,0:T(8,128)(2,1)}, s32[48]{0:T(128)}, /*index=5*/f32[16,128]{...) while((s32[]{:T(128)}, f32[16,128]{1,0:T(8,128)S(1)}, s32[48]{0:T(128)}, ...), condition=%wide.region_10.12_spmd, body=%wide.region_8.11_spmd.sunk | while | flops 3153094 | bytes 595087 | solution.py:36
  67.5 1.9 fusion.141
  73.0 1.9 fusion.141
  78.4 1.9 fusion.141
  81.8 8.2 %psum.51 = f32[16,128]{1,0:T(8,128)S(1)} all-reduce(f32[16,128]{1,0:T(8,128)S(1)} %get-tuple-element.863), channel_id=1, replica_groups=mesh['term'=8,'doc'=4] {'doc'}, use_global_device_ids=true, to_apply=%region_11.13 | all-reduce | flops 2048 | bytes 16384 | tf_op jit(solution)/shard_map/psum | solution.py:102
  90.1 15.1 %while.98 = (s32[]{:T(128)}, f32[16,128]{1,0:T(8,128)S(1)}, s32[48]{0:T(128)}, bf16[48,128,128]{2,1,0:T(8,128)(2,1)}, s32[48]{0:T(128)}, /*index=5*/f32[16,128]{...) while((s32[]{:T(128)}, f32[16,128]{1,0:T(8,128)S(1)}, s32[48]{0:T(128)}, ...), condition=%wide.region_14.16_spmd, body=%wide.region_12.15_spmd.sunk | while | flops 3153094 | bytes 595087 | solution.py:36
  92.1 1.6 fusion.145
  97.2 1.6 fusion.145
  105.2 13.9 %psum.52 = f32[16,128]{1,0:T(8,128)S(1)} all-reduce(f32[16,128]{1,0:T(8,128)S(1)} %get-tuple-element.864), channel_id=1, replica_groups=mesh['term'=8,'doc'=4] {'term'}, use_global_device_ids=true, to_apply=%region_15.17 | all-reduce | flops 2048 | bytes 16384 | tf_op jit(solution)/shard_map/psum | solution.py:105
  120.7 1.6 broadcast.307.clone
  122.3 28.9 %while.99 = (s32[]{:T(128)}, f32[16,128,256]{2,1,0:T(8,128)}, s32[48]{0:T(128)S(1)}, bf16[48,128,128]{2,1,0:T(8,128)(2,1)S(1)}, s32[48]{0:T(128)S(1)}, /*index=5...) while((s32[]{:T(128)}, f32[16,128,256]{2,1,0:T(8,128)}, ...), condition=%wide.region_18.0_spmd, body=%wide.region_16.20_spmd.sunk | while | flops 135791808 | bytes 12064447 | solution.py:36
  123.0 1.8 gather_fusion.4
  124.9 1.8 convolution_multiply_fusion.6
  126.8 5.4 scatter_fusion
  132.9 1.8 gather_fusion.4
  134.7 1.8 convolution_multiply_fusion.6
  136.6 5.2 scatter_fusion
  142.5 1.8 gather_fusion.4
  144.4 1.8 convolution_multiply_fusion.6
  146.2 5.0 scatter_fusion
  153.1 9.3 %while.100 = (s32[]{:T(128)}, f32[16,128]{1,0:T(8,128)S(1)}, s32[48]{0:T(128)S(1)}, bf16[48,128,128]{2,1,0:T(8,128)(2,1)S(1)}, s32[48]{0:T(128)S(1)}, /*index=5*...) while((s32[]{:T(128)}, f32[16,128]{1,0:T(8,128)S(1)}, ...), condition=%wide.region_22.25_spmd, body=%wide.region_20.24_spmd.sunk | while | flops 3153094 | bytes 595087 | solution.py:36
  162.4 9.6 %all-reduce.2 = (f32[256]{0:T(256)S(1)}, f32[2048]{0:T(1024)S(1)}) all-reduce(f32[256]{0:T(256)S(1)} %get-tuple-element.1039, f32[2048]{0:T(1024)S(1)} %bitcast.157), channel_id=1, replica_groups=mesh['term'=8,'doc'=4] {'doc'}, use_global_device_ids=true, to_apply=%region_25.28 | all-reduce | flops 2304 | bytes 18432 | tf_op jit(solution)/shard_map/psum | solution.py:100
  172.1 12.6 %reduce-scatter.3.cloned.1.call-done = f32[512,256]{1,0:T(8,128)} async-done(((f32[2048,256]{1,0:T(8,128)}), f32[512,256]{1,0:T(8,128)}) %reduce-scatter.3.cloned.1.call-update) | async-done | bytes 524304 | tf_op jit(solution)/shard_map/reduce_scatter | solution.py:117
  184.7 3.2 convolution_multiply_fusion.3
  188.6 128.9 %all-reduce.5.cloned.1.call-done = f32[256,256]{0,1:T(8,128)} async-done(((f32[256,256]{0,1:T(8,128)}), f32[256,256]{0,1:T(8,128)}) %all-reduce.5.cloned.1.call-update) | async-done | bytes 262160 | tf_op jit(solution)/shard_map/psum | solution.py:126
  319.6 11.7 %cholesky.130 = f32[128,128]{1,0:T(8,128)S(1)} custom-call(f32[128,128]{1,0:T(8,128)S(1)} %cholesky.194), custom_call_target="Cholesky" | custom-call | tf_op jit(solution)/shard_map/jit(cholesky)/cholesky | solution.py:16
  331.3 9.8 %custom-call.13 = f32[1,128,128]{1,2,0:T(8,128)S(1)} custom-call(f32[1,128,128]{2,1,0:T(8,128)S(1)} %get-tuple-element.1048), custom_call_target="InvertDiagBlocksLowerTriangular" | custom-call | tf_op jit(solution)/shard_map/jit(cholesky)/cholesky | solution.py:16
  341.6 11.7 %cholesky.147 = f32[128,128]{1,0:T(8,128)S(1)} custom-call(f32[128,128]{1,0:T(8,128)S(1)} %convolution_subtract_fusion.3), custom_call_target="Cholesky" | custom-call | tf_op jit(solution)/shard_map/jit(cholesky)/cholesky | solution.py:16
  355.6 4.3 while.102
  359.9 19.7 %custom-call.14 = f32[2,128,128]{1,2,0:T(8,128)S(1)} custom-call(f32[2,128,128]{2,1,0:T(8,128)S(1)} %get-tuple-element.882), custom_call_target="InvertDiagBlocksLowerTriangular" | custom-call | tf_op jit(solution)/shard_map/jit(_solve_triangular)/triangular_solve | solution.py:18
  380.4 2.4 fusion.87
  382.9 25.6 %all-gather.5.cloned.1.call-done = bf16[2048,256]{1,0:T(8,128)(2,1)} async-done(((bf16[512,256]{1,0:T(8,128)(2,1)}), bf16[2048,256]{1,0:T(8,128)(2,1)}) %all-gather.5.cloned.1.call-update) | async-done | bytes 1048592 | tf_op jit(solution)/shard_map/all_gather | solution.py:130
  408.6 2.5 multiply_convert_fusion
  411.1 1.6 broadcast.307
  412.7 29.1 %while.101 = (s32[]{:T(128)}, f32[16,128,256]{2,1,0:T(8,128)}, s32[48]{0:T(128)S(1)}, bf16[48,128,128]{2,1,0:T(8,128)(2,1)S(1)}, s32[48]{0:T(128)S(1)}, /*index=...) while((s32[]{:T(128)}, f32[16,128,256]{2,1,0:T(8,128)}, ...), condition=%wide.region_33.38_spmd, body=%wide.region_31.37_spmd.sunk | while | flops 135791808 | bytes 12064447 | solution.py:36
  413.4 1.8 gather_fusion.6
  415.3 1.8 convolution_multiply_fusion.7
  417.2 5.4 scatter_fusion.1
  423.3 1.8 gather_fusion.6
  425.1 1.8 convolution_multiply_fusion.7
  427.0 5.1 scatter_fusion.1
  432.8 1.8 gather_fusion.6
  434.7 1.8 convolution_multiply_fusion.7
  436.6 5.2 scatter_fusion.1
  442.3 40.0 %psum.55 = f32[256]{0:T(256)S(1)} all-reduce(f32[256]{0:T(256)S(1)} %bitcast.159), channel_id=1, replica_groups=mesh['term'=8,'doc'=4] {'term','doc'}, use_global_device_ids=true, to_apply=%region_35.40 | all-reduce | flops 256 | bytes 2048 | tf_op jit(solution)/shard_map/psum | solution.py:129
  482.2 2.4 convolution_multiply_fusion.2
  484.9 77.8 %all-gather.9.cloned.1.call-done = f32[8192,256]{1,0:T(8,128)} async-done(((f32[256,256]{1,0:T(8,128)}), f32[8192,256]{1,0:T(8,128)}) %all-gather.9.cloned.1.call-update) | async-done | bytes 8388624 | tf_op jit(solution)/shard_map/all_gather | solution.py:142
  562.7 3.9 reduce_sum.19
  566.8 11.7 %cholesky.164 = f32[128,128]{1,0:T(8,128)S(1)} custom-call(f32[128,128]{1,0:T(8,128)S(1)} %cholesky.197), custom_call_target="Cholesky" | custom-call | tf_op jit(solution)/shard_map/jit(cholesky)/cholesky | solution.py:16
  578.6 9.8 %custom-call.15 = f32[1,128,128]{1,2,0:T(8,128)S(1)} custom-call(f32[1,128,128]{2,1,0:T(8,128)S(1)} %get-tuple-element.1044), custom_call_target="InvertDiagBlocksLowerTriangular" | custom-call | tf_op jit(solution)/shard_map/jit(cholesky)/cholesky | solution.py:16
  588.9 11.7 %cholesky.181 = f32[128,128]{1,0:T(8,128)S(1)} custom-call(f32[128,128]{1,0:T(8,128)S(1)} %convolution_subtract_fusion.2), custom_call_target="Cholesky" | custom-call | tf_op jit(solution)/shard_map/jit(cholesky)/cholesky | solution.py:16
  603.4 4.4 while.103
  607.8 19.7 %custom-call.16 = f32[2,128,128]{1,2,0:T(8,128)S(1)} custom-call(f32[2,128,128]{2,1,0:T(8,128)S(1)} %get-tuple-element.883), custom_call_target="InvertDiagBlocksLowerTriangular" | custom-call | tf_op jit(solution)/shard_map/jit(_solve_triangular)/triangular_solve | solution.py:18
  629.5 21.0 %all-gather.7.cloned.1.call-done = bf16[2048,256]{1,0:T(8,128)(2,1)} async-done(((bf16[256,256]{1,0:T(8,128)(2,1)}), bf16[2048,256]{1,0:T(8,128)(2,1)}) %all-gather.7.cloned.1.call-update) | async-done | bytes 1048592 | tf_op jit(solution)/shard_map/all_gather | solution.py:149
  (210 shorter events, 80.7 us)
Async XLA Ops:
  7.2 177.6 %reduce-scatter.3.cloned.1.call-start = ((), (), s32[]{:S(2)}) async-start(), calls=%async_computation.2 | async-start | bytes 2621440 | tf_op jit(solution)/shard_map/reduce_scatter | solution.py:117
  65.4 53.8 %copy-start.4 = (bf16[2048,256]{1,0:T(8,128)(2,1)S(1)}, bf16[2048,256]{1,0:T(8,128)(2,1)}, u32[]{:S(2)}) copy-start(bf16[2048,256]{1,0:T(8,128)(2,1)} %param.30) | copy-start | bytes 3145732
  90.0 318.5 %copy-start.7 = (f32[2048]{0:T(1024)}, f32[2048]{0:T(1024)S(1)}, u32[]{:S(2)}) copy-start(f32[2048]{0:T(1024)S(1)} %get-tuple-element.1721) | copy-start | bytes 24580
  119.1 322.7 %copy-start.8 = (f32[2048]{0:T(1024)}, f32[2048]{0:T(1024)S(1)}, u32[]{:S(2)}) copy-start(f32[2048]{0:T(1024)S(1)} %get-tuple-element.1722) | copy-start | bytes 24580
  119.2 3.1 copy-start
  119.2 3.1 copy-start.5
  119.2 3.1 copy-start.6
  151.2 0.7 copy-start.9
  151.3 166.2 %all-reduce.5.cloned.1.call-start = ((), (), s32[]{:S(2)}) async-start(), calls=%async_computation.3 | async-start | bytes 524288 | tf_op jit(solution)/shard_map/psum | solution.py:126
  188.0 220.6 %all-gather.5.cloned.1.call-start = ((), (), s32[]{:S(2)}) async-start(), calls=%async_computation.4 | async-start | bytes 1310720 | tf_op jit(solution)/shard_map/all_gather | solution.py:130
  382.9 99.3 %reduce-scatter.5.cloned.1.call-start = ((), (), s32[]{:S(2)}) async-start(), calls=%async_computation.5 | async-start | bytes 2359296 | tf_op jit(solution)/shard_map/reduce_scatter | solution.py:138
  441.8 120.8 %all-gather.9.cloned.1.call-start = ((), (), s32[]{:S(2)}) async-start(), calls=%async_computation.7 | async-start | bytes 8650752 | tf_op jit(solution)/shard_map/all_gather | solution.py:142
  484.7 165.8 %all-gather.7.cloned.1.call-start = ((), (), s32[]{:S(2)}) async-start(), calls=%async_computation.6 | async-start | bytes 1179648 | tf_op jit(solution)/shard_map/all_gather | solution.py:149
  566.8 61.6 %copy-start.3 = (f32[256,256]{1,0:T(8,128)S(1)}, f32[256,256]{1,0:T(8,128)}, u32[]{:S(2)}) copy-start(f32[256,256]{1,0:T(8,128)} %reduce-scatter.5.cloned.1.call-done) | copy-start | bytes 786436
  578.6 71.9 %copy-start.1 = (bf16[2048,256]{1,0:T(8,128)(2,1)S(1)}, bf16[2048,256]{1,0:T(8,128)(2,1)}, u32[]{:S(2)}) copy-start(bf16[2048,256]{1,0:T(8,128)(2,1)} %all-gather.5.cloned.1.call-done) | copy-start | bytes 3145732
  650.5 1.6 copy-start.2
Sparse Core Ops, SparseCore 0:
  151.4 33.2 reduce-scatter.2
  190.8 126.6 all-reduce.4
  383.0 25.5 all-gather.4
  442.0 36.4 reduce-scatter.4
  484.8 77.8 all-gather.8
  629.6 20.8 all-gather.6
